TPU v7x, 32 devices: a whole 2x2x4 slice. The times are simulated.
32 devices in a mesh: dp: 4 (over z), mp: 8 (over y, x, core).
Axes of the slice: x: 2, y: 2, z: 4, core: 2. Of those that a mesh axis runs over, the one named last changes fastest.
Arguments:
- features: bfloat16 [192, 1664], P('dp'), may hold values from -6 to 6
- output_grad: bfloat16 [192, 1664], P('dp'), may hold values from -6 to 6
- send_rows: int32 [16, 12], P('dp'), may hold values from 0 to 48, as said below
- patches: int32 [16], replicated, may hold values from 0 to 12, as said below
- up_weight: float32 [6144, 1664], P(('dp', 'mp'))
- down_weight: float32 [6144, 1664], P(('dp', 'mp'))
- up_moment: float32 [6144, 1664], P(('dp', 'mp')), may hold values from -0.0006 to 0.0006
- down_moment: float32 [6144, 1664], P(('dp', 'mp')), may hold values from -0.0006 to 0.0006
- up_second: float32 [6144, 1664], P(('dp', 'mp')), may hold values from 1e-09 to 1e-07
- down_second: float32 [6144, 1664], P(('dp', 'mp')), may hold values from 1e-09 to 1e-07
Outputs:
- new_up: float32 [6144, 1664], P(('dp', 'mp'))
- new_down: float32 [6144, 1664], P(('dp', 'mp'))
- ratios: float32 [2], replicated
Inputs may be any that keep to these rules, and one draw needn't show every extreme that they name: `send_rows`: row d * 4 + p lists the rows of group d's block sent to group p, one a slot, 48 marking an empty slot. Group d's live rows are the first ones of its block, as many as the sum of its 4 patch counts; each live row is listed exactly once in group d's rows and no other row is listed. In every draw some group fills all its slots. `patches`: entries d * 4 to d * 4 + 3 are the patch counts of group d's images, 0 for an empty place; in every draw some group's counts sum to 48.
All inputs are finite; a program needn't handle non-finite values.
Results may differ from a plain program's by a relative error of at most 0.0003.
Values may be sent and summed in bfloat16 or wider, within the bound.
No kernel may reach another device: no remote copies, remote signals or barrier semaphores. Data moves between devices by JAX's collectives and lax.ppermute only.
A program may use at most 64 MiB of HBM per device.

v0:
```python
import math
import jax
import jax.numpy as jnp
from jax import lax
from jax.sharding import PartitionSpec as P

FF = 6144
IMGS = 4
inv_root_two = 1.0 / math.sqrt(2.0)
inv_root_tau = 1.0 / math.sqrt(2.0 * math.pi)
beta_first = 0.9
beta_second = 0.999
corr_first = 0.99997343860111
corr_second = 0.09520785288629
adam_eps = 1e-06
norm_eps = 1e-06
decay_rate = 0.05
learn_rate = 0.02


def gelu_exact(value):
    return 0.5 * value * (1.0 + lax.erf(value * inv_root_two))


def gelu_slope(value):
    return (
        0.5 * (1.0 + lax.erf(value * inv_root_two))
        + value * jnp.exp(-0.5 * value * value) * inv_root_tau
    )


def lamb_update(weight, grad, moment, second):
    moment_new = beta_first * moment + (1.0 - beta_first) * grad
    second_new = beta_second * second + (1.0 - beta_second) * grad * grad
    return (
        moment_new / corr_first / (jnp.sqrt(second_new / corr_second) + adam_eps)
        + decay_rate * weight
    )


def per_device(
    features,
    output_grad,
    send_rows,
    patches,
    up_weight,
    down_weight,
    up_moment,
    down_moment,
    up_second,
    down_second,
):
    width = features.shape[1]
    total = jnp.sum(patches).astype(jnp.float32)
    up_scale = 1.0 / math.sqrt(width)
    down_scale = 1.0 / math.sqrt(FF)
    group = lax.axis_index("dp")
    counts = lax.dynamic_slice_in_dim(patches, group * IMGS, IMGS)
    live = jnp.sum(counts)
    inside = (jnp.arange(features.shape[0], dtype=jnp.int32) < live)[:, None]
    inputs = jnp.where(inside, features, jnp.zeros_like(features))
    cotangent = jnp.where(inside, output_grad, jnp.zeros_like(output_grad))
    stacked = jnp.stack([up_weight.astype(jnp.bfloat16), down_weight.astype(jnp.bfloat16)])
    piece = lax.all_gather(stacked, "dp", axis=1, tiled=True)
    pre_part = (
        lax.dot_general(
            inputs, piece[0], (((1,), (1,)), ((), ())), preferred_element_type=jnp.float32
        )
        * up_scale
    )
    back_part = (
        lax.dot_general(
            cotangent, piece[1], (((1,), (1,)), ((), ())), preferred_element_type=jnp.float32
        )
        * down_scale
    )
    both = jnp.stack([pre_part, back_part])
    pre = both[0]
    hidden = gelu_exact(pre).astype(jnp.bfloat16)
    slope = (both[1] * gelu_slope(pre)).astype(jnp.bfloat16)
    up_term = lax.dot_general(
        slope, inputs, (((0,), (0,)), ((), ())), preferred_element_type=jnp.float32
    ) * (up_scale / total)
    down_term = lax.dot_general(
        hidden, cotangent, (((0,), (0,)), ((), ())), preferred_element_type=jnp.float32
    ) * (down_scale / total)
    summed = lax.psum_scatter(
        jnp.concatenate([up_term, down_term], 1).astype(jnp.bfloat16),
        "dp",
        scatter_dimension=0,
        tiled=True,
    ).astype(jnp.float32)
    update_up = lamb_update(up_weight, summed[:, :width], up_moment, up_second)
    update_down = lamb_update(down_weight, summed[:, width:], down_moment, down_second)
    weight_up_sq, update_up_sq, weight_down_sq, update_down_sq = lax.psum(
        (
            jnp.sum(up_weight * up_weight),
            jnp.sum(update_up * update_up),
            jnp.sum(down_weight * down_weight),
            jnp.sum(update_down * update_down),
        ),
        ("dp", "mp"),
    )
    ratio_up = jnp.sqrt(weight_up_sq / (update_up_sq + norm_eps))
    ratio_down = jnp.sqrt(weight_down_sq / (update_down_sq + norm_eps))
    new_up = up_weight - learn_rate * ratio_up * update_up
    new_down = down_weight - learn_rate * ratio_down * update_down
    return (new_up, new_down, jnp.stack([ratio_up, ratio_down]))


def solution(mesh):
    placed = (
        P("dp", None),
        P("dp", None),
        P("dp", None),
        P(),
        P(("dp", "mp"), None),
        P(("dp", "mp"), None),
        P(("dp", "mp"), None),
        P(("dp", "mp"), None),
        P(("dp", "mp"), None),
        P(("dp", "mp"), None),
    )
    return jax.shard_map(
        per_device,
        mesh=mesh,
        in_specs=placed,
        out_specs=(P(("dp", "mp"), None), P(("dp", "mp"), None), P()),
        check_vma=False,
    )
```

profile of v0, /device:TPU:0, one launch (start us, length us, event | category | flops | bytes accessed | tf_op | source)
XLA Modules:
  0.0 275.2 jit_solution(15147655237037164146)
XLA Ops:
  7.2 0.0 all-gather.2.cloned.1.call-start
  7.2 1.8 convert_bitcast_fusion
  9.0 1.2 pad_maximum_fusion.1
  10.2 0.0 all-gather.2.cloned.1.call-update
  10.2 0.0 reduce-scatter.2.cloned.1.call-start
  10.3 0.6 copy-done.6
  10.9 0.6 reduce_sum.56
  12.2 0.7 dynamic-slice_reduce_fusion
  12.9 0.6 iota_compare_fusion
  13.6 0.0 copy-start.4
  13.6 95.4 %all-gather.2.cloned.1.call-done = bf16[2,768,1664]{2,1,0:T(8,128)(2,1)} async-done(((bf16[2,192,1664]{2,1,0:T(8,128)(2,1)}), bf16[2,768,1664]{2,1,0:T(8,128)(2,1)}) %all-gather.2.cloned.1.call-update) | async-done | bytes 5111824 | tf_op jit(solution)/shard_map/all_gather | solution.py:64
  109.0 0.0 copy-done.5
  109.0 2.5 fusion
  111.5 0.0 copy-done.4
  111.6 0.9 multiply_convert_fusion
  112.5 5.3 %multiply_convert_fusion.1 = bf16[768,1664]{1,0:T(8,128)(2,1)} fusion(f32[]{:T(128)S(6)} %div.30, bf16[2,768,1664]{2,1,0:T(8,128)(2,1)} %all-gather.2.cloned.1.call-done, f32[48,768]{1,0:T(8,128)S(1)} %fusion, bf16[48,1664]{1,0:T(8,128)(2,1)S(1)} %copy-done.4, pred[48]{0:T(512)(128)(4,1)S(1)} %iota_compare_fusion, bf16[48,1664]{1,0:T(8,128)(2,1)S(1)} %copy-done.5), kind=kOutput, calls=%fused_computation.2 | convolution fusion | flops 248524800 | bytes 5579780 | tf_op jit(solution)/shard_map/dot_general | solution.py:81
  117.8 4.3 %pad_maximum_fusion = bf16[768,3328]{1,0:T(8,128)(2,1)} fusion(bf16[768,1664]{1,0:T(8,128)(2,1)S(1)} %multiply_convert_fusion, bf16[768,1664]{1,0:T(8,128)(2,1)} %multiply_convert_fusion.1), kind=kLoop, calls=%fused_computation | loop fusion | flops 10223616 | bytes 10223616 | tf_op jit(solution)/shard_map/concatenate | solution.py:88
  122.1 0.0 reduce-scatter.2.cloned.1.call-update
  122.1 0.0 copy-start
  122.1 0.0 copy-start.1
  122.2 90.1 %reduce-scatter.2.cloned.1.call-done = bf16[192,3328]{1,0:T(8,128)(2,1)} async-done(((bf16[768,3328]{1,0:T(8,128)(2,1)}), bf16[192,3328]{1,0:T(8,128)(2,1)}) %reduce-scatter.2.cloned.1.call-update) | async-done | bytes 1277968 | tf_op jit(solution)/shard_map/reduce_scatter | solution.py:87
  212.3 1.6 convert_element_type.24
  213.9 0.0 copy-done
  213.9 0.0 copy-done.1
  213.9 0.1 copy-done.3
  214.0 6.3 %multiply_reduce_fusion = (f32[]{:T(128)}, f32[192,1664]{1,0:T(8,128)}, f32[]{:T(128)}, f32[192,1664]{1,0:T(8,128)}, f32[]{:T(128)}, /*index=5*/f32[]{:T(128)}) fusion(f32[192,1664]{1,0:T(8,128)S(1)} %copy-done.1, f32[192,1664]{1,0:T(8,128)S(1)} %copy-done.3, f32[192,3328]{1,0:T(8,128)S(1)} %convert_element_type.24, f32[192,1664]{1,0:T(8,128)} %param.16, ...), kind=kLoop, calls=%fused_computation.23 | loop fusion | flops 10862588 | bytes 12779536 | tf_op jit(solution)/shard_map/reduce_sum | solution.py:100
  220.3 41.0 %all-reduce = (f32[]{:T(128)}, f32[]{:T(128)}, f32[]{:T(128)}, f32[]{:T(128)}) all-reduce(f32[]{:T(128)} %get-tuple-element.13, f32[]{:T(128)} %get-tuple-element.11, f32[]{:T(128)} %get-tuple-element.14, f32[]{:T(128)} %get-tuple-element.7), channel_id=1, replica_groups=mesh['dp'=4,'mp'=8] {'dp','mp'}, use_global_device_ids=true, to_apply=%region_1.0 | all-reduce | flops 4 | bytes 32 | tf_op jit(solution)/shard_map/psum | solution.py:95
  263.9 0.0 copy-start.2
  263.9 2.6 multiply_subtract_fusion.1
  266.5 0.0 copy-done.2
  266.5 1.3 multiply_subtract_fusion
  267.8 0.6 pad_maximum_fusion.2
  (3 shorter events, 0.0 us)
Async XLA Ops:
  7.2 101.8 %all-gather.2.cloned.1.call-start = ((), (), s32[]{:S(2)}) async-start(), calls=%async_computation.1 | async-start | bytes 6389760 | tf_op jit(solution)/shard_map/all_gather | solution.py:64
  10.2 0.7 copy-start.6
  10.2 98.8 %copy-start.5 = (bf16[48,1664]{1,0:T(8,128)(2,1)S(1)}, bf16[48,1664]{1,0:T(8,128)(2,1)}, u32[]{:S(2)}) copy-start(bf16[48,1664]{1,0:T(8,128)(2,1)} %param.10) | copy-start | bytes 479236
  10.2 202.1 %reduce-scatter.2.cloned.1.call-start = ((), (), s32[]{:S(2)}) async-start(), calls=%async_computation.2 | async-start | bytes 6389760 | tf_op jit(solution)/shard_map/reduce_scatter | solution.py:87
  13.6 98.0 %copy-start.4 = (bf16[48,1664]{1,0:T(8,128)(2,1)S(1)}, bf16[48,1664]{1,0:T(8,128)(2,1)}, u32[]{:S(2)}) copy-start(bf16[48,1664]{1,0:T(8,128)(2,1)} %param.11) | copy-start | bytes 479236
  122.1 91.8 %copy-start = (f32[192,1664]{1,0:T(8,128)S(1)}, f32[192,1664]{1,0:T(8,128)}, u32[]{:S(2)}) copy-start(f32[192,1664]{1,0:T(8,128)} %param.13) | copy-start | bytes 3833860
  122.1 91.7 %copy-start.1 = (f32[192,1664]{1,0:T(8,128)S(1)}, f32[192,1664]{1,0:T(8,128)}, u32[]{:S(2)}) copy-start(f32[192,1664]{1,0:T(8,128)} %param.14) | copy-start | bytes 3833860
  212.3 1.7 copy-start.3
  263.9 2.6 copy-start.2
Sparse Core Ops, SparseCore 0:
  10.4 98.5 all-gather.1
  122.3 90.0 reduce-scatter.1
where the time goes:
time: 276 us; the launch traced here: 275 us
  waiting for transfers between devices  186 us (67%)
  blocking collectives  41 us (15%)
  other arithmetic  21.6 us (8%)
  between operations  17.5 us (6%)
  matrix products  8.74 us (3%)
    all_gather x1, waiting for transfers between devices, per_device(): piece = lax.all_gather(stacked, 'dp', axis=1, tiled=True)  95.4 us
    reduce_scatter x1, waiting for transfers between devices, per_device(): lax.psum_scatter(jnp.concatenate([up_term, down_term], 1).astype(jnp.bflo...  90.1 us
    psum x1, blocking collectives, per_device(): lax.psum((jnp.sum(up_weight * up_weight), jnp.sum(update_up * update_up),...  41 us
    reduce_sum x1, other arithmetic, per_device(): jnp.sum(update_down * update_down)  6.27 us
  transfers between devices with their start and end apart: 2, of which 2 were waited for; matrix products, arithmetic and copies ran while one was open for 1% of the time, Pallas kernels for 0%

commit v1 on v0

--- a/solution.py
+++ b/solution.py
@@ -61,7 +61,12 @@
     inputs = jnp.where(inside, features, jnp.zeros_like(features))
     cotangent = jnp.where(inside, output_grad, jnp.zeros_like(output_grad))
     stacked = jnp.stack([up_weight.astype(jnp.bfloat16), down_weight.astype(jnp.bfloat16)])
-    piece = lax.all_gather(stacked, "dp", axis=1, tiled=True)
+    ring = [stacked]
+    for hop in range(3):
+        ring.append(lax.ppermute(ring[-1], "dp", [(dev, (dev + 1) % 4) for dev in range(4)]))
+    piece = jnp.roll(
+        jnp.concatenate(ring[::-1], axis=1), (lax.axis_index("dp") + 1) * ring[0].shape[1], axis=1
+    )
     pre_part = (
         lax.dot_general(
             inputs, piece[0], (((1,), (1,)), ((), ())), preferred_element_type=jnp.float32

time: 276 us -> 279 us (1.011)
  local copies, waits for them, and re-layouts: 0.72 us -> 10.3 us
  waiting for transfers between devices: 186 us -> 179 us
  starting transfers between devices: 0.08 us -> 3.15 us
    all_gather x1 -> x0, waiting for transfers between devices: 95.4 us -> none  [per_device(): piece = lax.all_gather(stacked, 'dp', axis=1, tiled=True)]
    ppermute x0 -> x3, waiting for transfers between devices: none -> 89 us  [per_device(): lax.ppermute(ring[-1], 'dp', [(dev, (dev + 1) % 4) for dev in range(4)])]
    unnamed x14 -> x22, local copies, waits for them, and re-layouts: 0.72 us -> 10.3 us
    ppermute x0 -> x3, starting transfers between devices: none -> 3.11 us  [per_device(): lax.ppermute(ring[-1], 'dp', [(dev, (dev + 1) % 4) for dev in range(4)])]
  transfers between devices with their start and end apart: 2 -> 4, of which waited for: 2 -> 4; matrix products, arithmetic and copies ran while one was open for 1% -> 1% of each run, Pallas kernels for 0% -> 0%
where the time goes in v1:
time: 279 us; the launch traced here: 278 us
  waiting for transfers between devices  179 us (64%)
  blocking collectives  41 us (15%)
  other arithmetic  20.9 us (7%)
  between operations  17.5 us (6%)
  local copies, waits for them, and re-layouts  10.3 us (4%)
  matrix products  7.05 us (3%)
  starting transfers between devices  3.15 us (1%)
    reduce_scatter x1, waiting for transfers between devices, per_device(): lax.psum_scatter(jnp.concatenate([up_term, down_term], 1).astype(jnp.bflo...  89.6 us
    ppermute x3, waiting for transfers between devices, per_device(): lax.ppermute(ring[-1], 'dp', [(dev, (dev + 1) % 4) for dev in range(4)])  89 us
    psum x1, blocking collectives, per_device(): lax.psum((jnp.sum(up_weight * up_weight), jnp.sum(update_up * update_up),...  41 us
    unnamed x22, local copies, waits for them, and re-layouts  10.3 us
    reduce_sum x1, other arithmetic, per_device(): jnp.sum(update_down * update_down)  6.27 us
  transfers between devices with their start and end apart: 4, of which 4 were waited for; matrix products, arithmetic and copies ran while one was open for 1% of the time, Pallas kernels for 0%

profile of v1, /device:TPU:0, one launch (start us, length us, event | category | flops | bytes accessed | tf_op | source)
XLA Modules:
  0.0 278.5 jit_solution(5057369126650512208)
XLA Ops:
  7.2 0.0 reduce-scatter.2.cloned.1.call-start
  7.2 1.8 convert_bitcast_fusion
  9.0 0.1 pad_maximum_fusion.1
  9.2 3.1 %collective-permute-start = (bf16[2,192,1664]{2,1,0:T(8,128)(2,1)S(1)}, bf16[2,192,1664]{2,1,0:T(8,128)(2,1)S(1)}, u32[]{:S(2)}, u32[]{:S(2)}) collective-permute-start(bf16[2,192,1664]{2,1,0:T(8,128)(2,1)S(1)} %pad_maximum_fusion.1), channel_id=1, source_target_pairs={{0,8},{8,16},{16,24},{24,0},{1,9},{9,17},{17,25},{25,1},{2,10},{10... | collective-permute-start | bytes 3833864 | tf_op jit(solution)/shard_map/ppermute | solution.py:66
  12.3 30.1 %collective-permute-done = bf16[2,192,1664]{2,1,0:T(8,128)(2,1)S(1)} collective-permute-done((bf16[2,192,1664]{2,1,0:T(8,128)(2,1)S(1)}, bf16[2,192,1664]{2,1,0:T(8,128)(2,1)S(1)}, u32[]{:S(2)}, u32[]{:S(2)}) %collective-permute-start) | collective-permute-done | bytes 1277984 | tf_op jit(solution)/shard_map/ppermute | solution.py:66
  42.4 31.1 %collective-permute-done.1 = bf16[2,192,1664]{2,1,0:T(8,128)(2,1)} collective-permute-done((bf16[2,192,1664]{2,1,0:T(8,128)(2,1)S(1)}, bf16[2,192,1664]{2,1,0:T(8,128)(2,1)}, u32[]{:S(2)}, u32[]{:S(2)}) %collective-permute-start.1) | collective-permute-done | bytes 1277984 | tf_op jit(solution)/shard_map/ppermute | solution.py:66
  73.5 0.6 reduce_sum.56
  74.2 0.7 dynamic-slice_reduce_fusion
  75.6 0.7 iota_compare_fusion
  76.3 27.8 %collective-permute-done.2 = bf16[2,192,1664]{2,1,0:T(8,128)(2,1)} collective-permute-done((bf16[2,192,1664]{2,1,0:T(8,128)(2,1)}, bf16[2,192,1664]{2,1,0:T(8,128)(2,1)}, u32[]{:S(2)}, u32[]{:S(2)}) %collective-permute-start.2) | collective-permute-done | bytes 1277984 | tf_op jit(solution)/shard_map/ppermute | solution.py:66
  104.0 1.4 constant_dynamic-update-slice_fusion.7
  105.4 1.5 constant_dynamic-update-slice_fusion.6
  106.9 0.2 constant_dynamic-update-slice_fusion.5
  107.1 0.2 constant_dynamic-update-slice_fusion.4
  107.3 1.5 constant_dynamic-update-slice_fusion.3
  108.8 1.5 constant_dynamic-update-slice_fusion.2
  110.3 0.2 constant_dynamic-update-slice_fusion.1
  110.5 0.2 constant_dynamic-update-slice_fusion
  110.7 3.9 %copy-done.3 = bf16[2,1536,1664]{2,1,0:T(8,128)(2,1)} copy-done((bf16[2,1536,1664]{2,1,0:T(8,128)(2,1)}, bf16[2,1536,1664]{2,1,0:T(8,128)(2,1)S(1)}, u32[]{:S(2)}) %copy-start.3) | copy-done | bytes 10223640
  114.5 0.8 fusion
  115.4 0.1 copy-done.6
  115.4 0.9 multiply_convert_fusion
  116.3 5.3 %multiply_convert_fusion.1 = bf16[768,1664]{1,0:T(8,128)(2,1)} fusion(f32[]{:T(128)S(6)} %div.30, bf16[2,1536,1664]{2,1,0:T(8,128)(2,1)} %copy-done.3, s32[]{:T(128)S(6)} %add.79, s32[]{:T(128)S(6)} %select_n.26, f32[48,768]{1,0:T(8,128)S(1)} %fusion, bf16[48,1664]{1,0:T(8,128)(2,1)S(1)} %copy-done.6, pred[48]{0:T(512)(128)(4,1)S(1)} %iota_compare_fusion, ...), kind=kOutput, calls=%fused_computation.2 | convolution fusion | flops 248524800 | bytes 5579788 | tf_op jit(solution)/shard_map/dot_general | solution.py:86
  121.7 4.3 %pad_maximum_fusion = bf16[768,3328]{1,0:T(8,128)(2,1)} fusion(bf16[768,1664]{1,0:T(8,128)(2,1)S(1)} %multiply_convert_fusion, bf16[768,1664]{1,0:T(8,128)(2,1)} %multiply_convert_fusion.1), kind=kLoop, calls=%fused_computation | loop fusion | flops 10223616 | bytes 10223616 | tf_op jit(solution)/shard_map/concatenate | solution.py:93
  126.0 89.6 %reduce-scatter.2.cloned.1.call-done = bf16[192,3328]{1,0:T(8,128)(2,1)} async-done(((bf16[768,3328]{1,0:T(8,128)(2,1)}), bf16[192,3328]{1,0:T(8,128)(2,1)}) %reduce-scatter.2.cloned.1.call-update) | async-done | bytes 1277968 | tf_op jit(solution)/shard_map/reduce_scatter | solution.py:92
  215.6 1.6 convert_element_type.24
  217.2 0.1 copy-done.4
  217.3 6.3 %multiply_reduce_fusion = (f32[]{:T(128)}, f32[192,1664]{1,0:T(8,128)}, f32[]{:T(128)}, f32[192,1664]{1,0:T(8,128)}, f32[]{:T(128)}, /*index=5*/f32[]{:T(128)}) fusion(f32[192,1664]{1,0:T(8,128)S(1)} %copy-done, f32[192,1664]{1,0:T(8,128)S(1)} %copy-done.4, f32[192,3328]{1,0:T(8,128)S(1)} %convert_element_type.24, f32[192,1664]{1,0:T(8,128)} %param.16, ...), kind=kLoop, calls=%fused_computation.23 | loop fusion | flops 10862588 | bytes 12779536 | tf_op jit(solution)/shard_map/reduce_sum | solution.py:105
  223.5 41.0 %all-reduce = (f32[]{:T(128)}, f32[]{:T(128)}, f32[]{:T(128)}, f32[]{:T(128)}) all-reduce(f32[]{:T(128)} %get-tuple-element.13, f32[]{:T(128)} %get-tuple-element.11, f32[]{:T(128)} %get-tuple-element.14, f32[]{:T(128)} %get-tuple-element.7), channel_id=1, replica_groups=mesh['dp'=4,'mp'=8] {'dp','mp'}, use_global_device_ids=true, to_apply=%region_1.0 | all-reduce | flops 4 | bytes 32 | tf_op jit(solution)/shard_map/psum | solution.py:100
  267.2 0.6 pad_maximum_fusion.2
  267.8 2.6 multiply_subtract_fusion
  270.4 1.3 multiply_subtract_fusion.1
  (16 shorter events, 0.1 us)
Async XLA Ops:
  7.2 208.4 %reduce-scatter.2.cloned.1.call-start = ((), (), s32[]{:S(2)}) async-start(), calls=%async_computation.1 | async-start | bytes 6389760 | tf_op jit(solution)/shard_map/reduce_scatter | solution.py:92
  9.0 64.5 %copy-start.7 = (s32[16]{0:T(128)S(1)}, s32[16]{0:T(128)}, u32[]{:S(2)}) copy-start(s32[16]{0:T(128)} %param.12) | copy-start | bytes 196
  9.2 33.2 %collective-permute-start = (bf16[2,192,1664]{2,1,0:T(8,128)(2,1)S(1)}, bf16[2,192,1664]{2,1,0:T(8,128)(2,1)S(1)}, u32[]{:S(2)}, u32[]{:S(2)}) collective-permute-start(bf16[2,192,1664]{2,1,0:T(8,128)(2,1)S(1)} %pad_maximum_fusion.1), channel_id=1, source_target_pairs={{0,8},{8,16},{16,24},{24,0},{1,9},{9,17},{17,25},{25,1},{2,10},{10... | collective-permute-start | bytes 3833864 | tf_op jit(solution)/shard_map/ppermute | solution.py:66
  42.4 31.1 %collective-permute-start.1 = (bf16[2,192,1664]{2,1,0:T(8,128)(2,1)S(1)}, bf16[2,192,1664]{2,1,0:T(8,128)(2,1)}, u32[]{:S(2)}, u32[]{:S(2)}) collective-permute-start(bf16[2,192,1664]{2,1,0:T(8,128)(2,1)S(1)} %collective-permute-done), channel_id=1, source_target_pairs={{0,8},{8,16},{16,24},{24,0},{1,9},{9,17},{17,25},{25,1},{2,10},{10... | collective-permute-start | bytes 3833864 | tf_op jit(solution)/shard_map/ppermute | solution.py:66
  73.5 30.5 %collective-permute-start.2 = (bf16[2,192,1664]{2,1,0:T(8,128)(2,1)}, bf16[2,192,1664]{2,1,0:T(8,128)(2,1)}, u32[]{:S(2)}, u32[]{:S(2)}) collective-permute-start(bf16[2,192,1664]{2,1,0:T(8,128)(2,1)} %collective-permute-done.1), channel_id=1, source_target_pairs={{0,8},{8,16},{16,24},{24,0},{1,9},{9,17},{17,25},{25,1},{2,10},{10... | collective-permute-start | bytes 3833864 | tf_op jit(solution)/shard_map/ppermute | solution.py:66
  110.4 4.1 %copy-start.5 = (bf16[48,1664]{1,0:T(8,128)(2,1)S(1)}, bf16[48,1664]{1,0:T(8,128)(2,1)}, u32[]{:S(2)}) copy-start(bf16[48,1664]{1,0:T(8,128)(2,1)} %param.10) | copy-start | bytes 479236
  110.6 3.9 %copy-start.3 = (bf16[2,1536,1664]{2,1,0:T(8,128)(2,1)}, bf16[2,1536,1664]{2,1,0:T(8,128)(2,1)S(1)}, u32[]{:S(2)}) copy-start(bf16[2,1536,1664]{2,1,0:T(8,128)(2,1)S(1)} %constant_dynamic-update-slice_fusion) | copy-start | bytes 30670852
  114.5 0.9 copy-start.6
  126.0 91.2 %copy-start = (f32[192,1664]{1,0:T(8,128)S(1)}, f32[192,1664]{1,0:T(8,128)}, u32[]{:S(2)}) copy-start(f32[192,1664]{1,0:T(8,128)} %param.14) | copy-start | bytes 3833860
  126.0 91.2 %copy-start.1 = (f32[192,1664]{1,0:T(8,128)S(1)}, f32[192,1664]{1,0:T(8,128)}, u32[]{:S(2)}) copy-start(f32[192,1664]{1,0:T(8,128)} %param.13) | copy-start | bytes 3833860
  215.6 1.7 copy-start.4
  267.8 2.6 copy-start.2
Sparse Core Ops, SparseCore 0:
  126.1 89.4 reduce-scatter.1
